TPU v7x, 128 devices: a whole 4x4x4 slice. The times are simulated.
128 devices in a mesh: slab: 4 (over y_hi, core), orb: 8 (over x, y_lo), pois: 4 (over z).
Axes of the slice: x: 4, y: 4 (y_hi: 2, y_lo: 2; y = y_hi * 2 + y_lo), z: 4, core: 2. Of those that a mesh axis runs over, the one named last changes fastest.
Arguments:
- orbitals: bfloat16 [32, 2, 192, 128, 128], P('orb', None, 'slab', 'pois'), may hold values from -8 to 8
- occupations: float32 [32], P('orb'), may hold values from 5e-05 to 0.0005
- ext_pot: float32 [192, 128, 128], P('slab', 'pois'), may hold values from -1 to 1
- hartree_old: float32 [192, 128, 128], P('slab', 'pois'), may hold values from 0 to 2
Outputs:
- orbitals_new: float32 [32, 2, 192, 128, 128], P('orb', None, 'slab', 'pois')
- hartree_new: float32 [192, 128, 128], P('slab', 'pois', 'orb')
All inputs are finite; a program needn't handle non-finite values.
Results may differ from a plain program's by a relative error of at most 0.0003.
Values may be sent and summed in bfloat16 or wider, within the bound.
No kernel may reach another device: no remote copies, remote signals or barrier semaphores. Data moves between devices by JAX's collectives and lax.ppermute only.
A program may use at most 64 MiB of HBM per device.

v0:
```python
import jax
import jax.numpy as jnp
from jax import lax
from jax.sharding import PartitionSpec as P

NX = 192
NY = 128
NZ = 128
time_step = 0.3


def extended(cells, sides, width):
    for axis, dim in sides:
        count = lax.axis_size(axis)
        ends = count - 1
        head = lax.slice_in_dim(cells, 0, width, axis=dim)
        tail = lax.slice_in_dim(cells, cells.shape[dim] - width, cells.shape[dim], axis=dim)
        cells = jnp.concatenate(
            [
                lax.ppermute(tail, axis, [(i, (i + 1) % count) for i in range(ends)]),
                cells,
                lax.ppermute(head, axis, [((i + 1) % count, i) for i in range(ends)]),
            ],
            axis=dim,
        )
    return cells


def sine_table(row_count, col_start, col_count, length):
    row_index = lax.iota(jnp.int32, row_count) + 1
    col_index = col_start + lax.iota(jnp.int32, col_count) + 1
    product = row_index[:, None] * col_index[None, :] % (2 * (length + 1))
    return jnp.sin(jnp.pi * product.astype(jnp.float32) / (length + 1))


def eigen_values(first_mode, mode_count, length):
    mode_index = first_mode + lax.iota(jnp.int32, mode_count) + 1
    return 2.0 - 2.0 * jnp.cos(jnp.pi * mode_index.astype(jnp.float32) / (length + 1))


def hamiltonian(padded, potential):
    center = padded[:, :, 1:-1, 1:-1, :].astype(jnp.float32)
    z_padded = jnp.pad(center, ((0, 0), (0, 0), (0, 0), (0, 0), (1, 1)))
    beside_all = padded[:, :, 2:, 1:-1, :].astype(jnp.float32) + padded[:, :, :-2, 1:-1, :].astype(
        jnp.float32
    )
    beside_all = (
        beside_all
        + padded[:, :, 1:-1, 2:, :].astype(jnp.float32)
        + padded[:, :, 1:-1, :-2, :].astype(jnp.float32)
    )
    beside_all = beside_all + z_padded[..., 2:] + z_padded[..., :-2]
    return (3.0 + potential) * center - 0.5 * beside_all


def plane_sine(spectrum):
    highest = lax.Precision.HIGHEST
    width_c, width_x, width_y = spectrum.shape
    slab_start = lax.axis_index("slab") * width_x
    pois_start = lax.axis_index("pois") * width_y
    sines_x = sine_table(NX, slab_start, width_x, NX)
    sines_y = sine_table(NY, pois_start, width_y, NY)
    partial_sum = jnp.einsum("ax,cxy->ayc", sines_x, spectrum, precision=highest)
    full_sum = jnp.einsum("by,ayc->abc", sines_y, partial_sum, precision=highest)
    row_blocks = full_sum.reshape(NX // width_x, width_x, NY // width_y, width_y, width_c)
    row_blocks = jnp.transpose(row_blocks, (0, 2, 1, 3, 4)).reshape(-1, width_c)
    result_rows = lax.psum_scatter(row_blocks, ("slab", "pois"), scatter_dimension=0, tiled=True)
    return result_rows.reshape(width_x, width_y, width_c)


def body(orbitals, occupations, ext_pot, hartree_old):
    highest = lax.Precision.HIGHEST
    width_x = orbitals.shape[2]
    width_y = orbitals.shape[3]
    padded = extended(orbitals, (("slab", 2), ("pois", 3)), 1)
    center = padded[:, :, 1:-1, 1:-1, :].astype(jnp.float32)

    def first_image(potential):
        image_one = hamiltonian(padded, potential)
        image_padded = extended(image_one, (("slab", 2), ("pois", 3)), 1)
        return (image_one, image_padded)

    def taylor_step(potential):
        image_one, image_padded = first_image(potential)
        image_two = hamiltonian(image_padded, potential)
        rotated = jnp.stack([image_one[:, 1], -image_one[:, 0]], axis=1)
        return center + time_step * rotated - 0.5 * time_step * time_step * image_two

    pot_start = ext_pot + hartree_old
    predicted = taylor_step(pot_start)
    density_part = jnp.sum(
        occupations[:, None, None, None]
        * (predicted[:, 0] * predicted[:, 0] + predicted[:, 1] * predicted[:, 1]),
        axis=0,
    )
    total = lax.psum(jnp.sum(density_part), ("slab", "orb", "pois"))
    density_part = density_part - total / (NX * NY * NZ) / lax.axis_size("orb")
    full_z = density_part.shape[2]
    width_z = full_z // lax.axis_size("orb")
    sines = sine_table(lax.axis_size("orb") * width_z, 0, full_z, full_z)
    spectrum = lax.psum_scatter(
        jnp.einsum("cz,xyz->cxy", sines, density_part, precision=highest),
        "orb",
        scatter_dimension=0,
        tiled=True,
    )
    spectrum = plane_sine(spectrum)
    slab_start = lax.axis_index("slab") * width_x
    pois_start = lax.axis_index("pois") * width_y
    orb_start = lax.axis_index("orb") * width_z
    divisor = (
        eigen_values(slab_start, width_x, NX)[:, None, None]
        + eigen_values(pois_start, width_y, NY)[None, :, None]
        + eigen_values(orb_start, width_z, NZ)[None, None, :]
    )
    factor = 32.0 * jnp.pi / ((NX + 1) * (NY + 1) * (NZ + 1))
    scaled = jnp.transpose(spectrum * factor / divisor, (2, 0, 1))
    field_part = plane_sine(scaled)
    section = lax.all_gather(field_part, "orb", axis=2, tiled=True)
    sines = sine_table(full_z, jnp.int32(0), section.shape[2], full_z)
    hartree_full = jnp.einsum("zc,xyc->xyz", sines, section, precision=highest)
    pot_middle = ext_pot + 0.5 * (hartree_old + hartree_full)
    orbitals_new = taylor_step(pot_middle)
    hartree_new = lax.dynamic_slice_in_dim(hartree_full, orb_start, width_z, 2)
    return (orbitals_new, hartree_new)


def solution(mesh):
    placed = (
        P("orb", None, "slab", "pois", None),
        P("orb"),
        P("slab", "pois", None),
        P("slab", "pois", None),
    )
    return jax.shard_map(
        body,
        mesh=mesh,
        in_specs=placed,
        out_specs=(P("orb", None, "slab", "pois", None), P("slab", "pois", "orb")),
        check_vma=False,
    )
```

profile of v0, /device:TPU:52, one launch (start us, length us, event | category | flops | bytes accessed | tf_op | source)
XLA Modules:
  0.0 538.2 jit_solution(13242921233021301441)
XLA Ops:
  7.2 3.3 fusion.118
  15.4 5.3 collective-permute-done.1
  20.7 3.8 collective-permute-start.3
  27.4 3.8 collective-permute-done.2
  31.3 10.8 %multiply_subtract_fusion.1 = (f32[4,2,48,32,128]{4,2,3,1,0:T(8,128)S(1)}, f32[4,2,48,32,128]{4,2,3,1,0:T(8,128)}) fusion(f32[48,32,128]{2,0,1:T(8,128)S(1)} %copy.45, bf16[4,2,48,32,128]{4,3,2,1,0:T(8,128)(2,1)S(1)} %copy-done.2, f32[4,2,48,32,128]{4,2,3,1,0:T(8,128)S(1)} %get-tuple-element.33, bf16[4,2,1,32,128]{4,2,3,1,0:T(2,128)(2,1)S(1)} %collective-permute-done, ...), kind=kLoop, calls=%fused_computation.48 | loop fusion | flops 51904512 | bytes 26288128 | tf_op jit(solution)/shard_map/sub | solution.py:53
  46.7 5.3 collective-permute-done.5
  52.1 3.5 collective-permute-start.7
  60.0 3.5 collective-permute-done.6
  63.5 9.9 %fusion.8 = f32[4,2,48,32,128]{4,2,3,1,0:T(8,128)S(1)} fusion(f32[4,2,48,32,128]{4,2,3,1,0:T(8,128)S(1)} %get-tuple-element.14, f32[4,2,50,1,128]{4,2,3,1,0:T(8,128)S(1)} %collective-permute-done.7, f32[4,2,1,32,128]{4,2,3,1,0:T(1,128)S(1)} %bitcast.73, f32[4,2,1,32,128]{4,2,3,1,0:T(1,128)S(1)} %bitcast.75, ...), kind=kLoop, calls=%fused_computation.14 | loop fusion | flops 34603008 | bytes 23478272 | tf_op jit(solution)/shard_map/sub | solution.py:87
  75.6 61.9 %psum.7 = f32[]{:T(128)} all-reduce(f32[]{:T(128)} %get-tuple-element.12), channel_id=1, replica_groups=mesh['slab'=4,'orb'=8,'pois'=4] {'slab','orb','pois'}, use_global_device_ids=true, to_apply=%region_2.3 | all-reduce | flops 1 | bytes 8 | tf_op jit(solution)/shard_map/psum | solution.py:96
  139.6 4.7 fusion.26
  144.4 51.7 %reduce-scatter.4.cloned.1.call-done = f32[16,48,32]{1,0,2:T(8,128)} async-done(((f32[128,48,32]{1,0,2:T(8,128)}), f32[16,48,32]{1,0,2:T(8,128)}) %reduce-scatter.4.cloned.1.call-update) | async-done | bytes 98320 | tf_op jit(solution)/shard_map/reduce_scatter | solution.py:101
  201.6 4.1 convolution_bitcast_fusion.1
  205.7 3.1 copy.61
  208.7 5.4 reshape.112
  214.1 7.1 %copy.62 = f32[4,4,48,32,16]{3,2,1,0,4:T(8,128)} copy(f32[4,4,48,32,16]{2,0,4,3,1:T(4,128)} %bitcast.66) | data formatting | bytes 3145728 | tf_op jit(solution)/shard_map/transpose | solution.py:66
  221.2 5.6 %reshape.113 = f32[24576,16]{0,1:T(8,128)} reshape(f32[4,4,48,32,16]{3,2,1,0,4:T(8,128)} %copy.62) | data formatting | bytes 3145728 | tf_op jit(solution)/shard_map/reshape | solution.py:66
  228.5 66.3 %reduce-scatter.6.cloned.1.call-done = f32[1536,16]{0,1:T(8,128)} async-done(((f32[24576,16]{0,1:T(8,128)}), f32[1536,16]{0,1:T(8,128)}) %reduce-scatter.6.cloned.1.call-update) | async-done | bytes 98320 | tf_op jit(solution)/shard_map/reduce_scatter | solution.py:67
  302.9 4.1 convolution_bitcast_fusion
  310.0 5.4 reshape.114
  315.3 7.1 %copy.66 = f32[4,4,48,32,16]{3,2,1,0,4:T(8,128)} copy(f32[4,4,48,32,16]{2,0,4,3,1:T(4,128)} %bitcast.67) | data formatting | bytes 3145728 | tf_op jit(solution)/shard_map/transpose | solution.py:66
  322.4 5.6 %reshape.115 = f32[24576,16]{0,1:T(8,128)} reshape(f32[4,4,48,32,16]{3,2,1,0,4:T(8,128)} %copy.66) | data formatting | bytes 3145728 | tf_op jit(solution)/shard_map/reshape | solution.py:66
  328.1 68.1 %reduce-scatter.8.cloned.1.call-done = f32[1536,16]{0,1:T(8,128)} async-done(((f32[24576,16]{0,1:T(8,128)}), f32[1536,16]{0,1:T(8,128)}) %reduce-scatter.8.cloned.1.call-update) | async-done | bytes 98320 | tf_op jit(solution)/shard_map/reduce_scatter | solution.py:67
  397.4 61.2 %all_gather.3 = f32[48,32,128]{1,2,0:T(8,128)S(1)} all-gather(f32[48,32,16]{1,2,0:T(8,128)S(1)} %copy.67), channel_id=1, replica_groups=mesh['slab'=4,'orb'=8,'pois'=4] {'orb'}, dimensions={2}, use_global_device_ids=true | all-gather | bytes 884736 | tf_op jit(solution)/shard_map/all_gather | solution.py:119
  458.6 7.4 %add_add_fusion = (f32[48,32,128]{2,1,0:T(8,128)S(1)}, f32[48,32,128]{2,1,0:T(8,128)}) fusion(f32[48,32,128]{2,1,0:T(8,128)} %param.6, f32[48,32,128]{2,1,0:T(8,128)} %param.7, f32[48,32,128]{1,2,0:T(8,128)S(1)} %all_gather.3, s32[128]{0:T(128)S(1)} %iota_add_fusion.1), kind=kOutput, calls=%fused_computation.71 | convolution fusion | flops 302923776 | bytes 3932672 | tf_op jit(solution)/shard_map/zc,xyc->xyz/dot_general | solution.py:121
  466.5 4.5 multiply_subtract_fusion
  474.7 4.9 collective-permute-start.8
  482.4 5.0 collective-permute-done.9
  491.2 4.8 collective-permute-start.10
  496.0 3.3 fusion.113
  502.8 24.1 %fusion.14 = f32[4,2,48,32,128]{4,2,3,1,0:T(8,128)S(1)} fusion(f32[4,2,48,32,128]{4,2,3,1,0:T(8,128)} %copy-done, f32[4,2,50,1,128]{4,2,3,1,0:T(8,128)} %collective-permute-done.11, f32[4,2,1,32,128]{4,2,3,1,0:T(1,128)S(1)} %bitcast.69, f32[4,2,1,32,128]{4,2,3,1,0:T(1,128)S(1)} %bitcast.71, f32[4,2,50,1,128]{4,2,3,1,0:T(8,128)} %collective-permute-done.10, ...), kind=kLoop, calls=%fused_computation.20 | loop fusion | flops 34603008 | bytes 23478272 | tf_op jit(solution)/shard_map/sub | solution.py:87
  526.9 4.6 copy.75
  (68 shorter events, 53.9 us)
Async XLA Ops:
  7.2 188.9 %reduce-scatter.4.cloned.1.call-start = ((), (), s32[]{:S(2)}) async-start(), calls=%async_computation.3 | async-start | bytes 2359296 | tf_op jit(solution)/shard_map/reduce_scatter | solution.py:101
  7.2 19.4 %copy-start.5 = (f32[48,32,128]{2,1,0:T(8,128)S(1)}, f32[48,32,128]{2,1,0:T(8,128)}, u32[]{:S(2)}) copy-start(f32[48,32,128]{2,1,0:T(8,128)} %param.6) | copy-start | bytes 2359300
  7.2 19.4 %copy-start.6 = (f32[48,32,128]{2,1,0:T(8,128)S(1)}, f32[48,32,128]{2,1,0:T(8,128)}, u32[]{:S(2)}) copy-start(f32[48,32,128]{2,1,0:T(8,128)} %param.7) | copy-start | bytes 2359300
  10.5 20.7 %copy-start.2 = (bf16[4,2,48,32,128]{4,3,2,1,0:T(8,128)(2,1)S(1)}, bf16[4,2,48,32,128]{4,3,2,1,0:T(8,128)(2,1)}, u32[]{:S(2)}) copy-start(bf16[4,2,48,32,128]{4,3,2,1,0:T(8,128)(2,1)} %param.4) | copy-start | bytes 9437188
  10.8 4.6 collective-permute-start
  12.9 7.8 %collective-permute-start.1 = (bf16[4,2,1,32,128]{4,2,3,1,0:T(2,128)(2,1)S(1)}, bf16[4,2,1,32,128]{4,2,3,1,0:T(2,128)(2,1)S(1)}, u32[]{:S(2)}, u32[]{:S(2)}) collective-permute-start(bf16[4,2,1,32,128]{4,2,3,1,0:T(2,128)(2,1)S(1)} %get-tuple-element.30), channel_id=1, source_target_pairs={{0,32},{32,64},{64,96},{1,33},{33,65},{65,97},{2,34},{34,66},{66,9... | collective-permute-start | bytes 196616 | tf_op jit(solution)/shard_map/ppermute | solution.py:20
  20.7 6.7 %collective-permute-start.3 = (bf16[4,2,50,1,128]{4,2,3,1,0:T(8,128)(2,1)S(1)}, bf16[4,2,50,1,128]{4,2,3,1,0:T(8,128)(2,1)S(1)}, u32[]{:S(2)}, u32[]{:S(2)}) collective-permute-start(bf16[4,2,50,1,128]{4,2,3,1,0:T(8,128)(2,1)S(1)} %get-tuple-element.29), channel_id=1, source_target_pairs={{0,1},{1,2},{2,3},{4,5},{5,6},{6,7},{8,9},{9,10},{10,11},{12,13},{... | collective-permute-start | bytes 307208 | tf_op jit(solution)/shard_map/ppermute | solution.py:20
  24.6 6.7 %collective-permute-start.2 = (bf16[4,2,50,1,128]{4,2,3,1,0:T(8,128)(2,1)S(1)}, bf16[4,2,50,1,128]{4,2,3,1,0:T(8,128)(2,1)S(1)}, u32[]{:S(2)}, u32[]{:S(2)}) collective-permute-start(bf16[4,2,50,1,128]{4,2,3,1,0:T(8,128)(2,1)S(1)} %get-tuple-element.28), channel_id=1, source_target_pairs={{1,0},{2,1},{3,2},{5,4},{6,5},{7,6},{9,8},{10,9},{11,10},{13,12},{... | collective-permute-start | bytes 307208 | tf_op jit(solution)/shard_map/ppermute | solution.py:22
  42.3 4.4 collective-permute-start.4
  44.2 7.8 %collective-permute-start.5 = (f32[4,2,1,32,128]{4,3,2,1,0:T(8,128)S(1)}, f32[4,2,1,32,128]{4,3,2,1,0:T(8,128)S(1)}, u32[]{:S(2)}, u32[]{:S(2)}) collective-permute-start(f32[4,2,1,32,128]{4,3,2,1,0:T(8,128)S(1)} %bitcast.77), channel_id=1, source_target_pairs={{0,32},{32,64},{64,96},{1,33},{33,65},{65,97},{2,34},{34,66},{66,9... | collective-permute-start | bytes 393224 | tf_op jit(solution)/shard_map/ppermute | solution.py:20
  52.1 7.9 %collective-permute-start.7 = (f32[4,2,50,1,128]{4,2,3,1,0:T(8,128)S(1)}, f32[4,2,50,1,128]{4,2,3,1,0:T(8,128)S(1)}, u32[]{:S(2)}, u32[]{:S(2)}) collective-permute-start(f32[4,2,50,1,128]{4,2,3,1,0:T(8,128)S(1)} %get-tuple-element.19), channel_id=1, source_target_pairs={{0,1},{1,2},{2,3},{4,5},{5,6},{6,7},{8,9},{9,10},{10,11},{12,13},{... | collective-permute-start | bytes 614408 | tf_op jit(solution)/shard_map/ppermute | solution.py:20
  55.6 7.9 %collective-permute-start.6 = (f32[4,2,50,1,128]{4,2,3,1,0:T(8,128)S(1)}, f32[4,2,50,1,128]{4,2,3,1,0:T(8,128)S(1)}, u32[]{:S(2)}, u32[]{:S(2)}) collective-permute-start(f32[4,2,50,1,128]{4,2,3,1,0:T(8,128)S(1)} %get-tuple-element.18), channel_id=1, source_target_pairs={{1,0},{2,1},{3,2},{5,4},{6,5},{7,6},{9,8},{10,9},{11,10},{13,12},{... | collective-permute-start | bytes 614408 | tf_op jit(solution)/shard_map/ppermute | solution.py:22
  63.5 10.0 %copy-start.7 = (f32[4]{0:T(128)S(1)}, f32[4]{0:T(128)}, u32[]{:S(2)}) copy-start(f32[4]{0:T(128)} %param.5) | copy-start | bytes 52
  144.3 150.5 %reduce-scatter.6.cloned.1.call-start = ((), (), s32[]{:S(2)}) async-start(), calls=%async_computation.4 | async-start | bytes 1671168 | tf_op jit(solution)/shard_map/reduce_scatter | solution.py:67
  226.8 169.4 %reduce-scatter.8.cloned.1.call-start = ((), (), s32[]{:S(2)}) async-start(), calls=%async_computation.5 | async-start | bytes 1671168 | tf_op jit(solution)/shard_map/reduce_scatter | solution.py:67
  466.5 4.6 copy-start.3
  471.1 2.7 copy-start
  474.7 7.7 %collective-permute-start.8 = (f32[4,2,1,32,128]{4,3,2,1,0:T(8,128)}, f32[4,2,1,32,128]{4,3,2,1,0:T(8,128)S(1)}, u32[]{:S(2)}, u32[]{:S(2)}) collective-permute-start(f32[4,2,1,32,128]{4,3,2,1,0:T(8,128)} %bitcast.17), channel_id=1, source_target_pairs={{32,0},{64,32},{96,64},{33,1},{65,33},{97,65},{34,2},{66,34},{98,6... | collective-permute-start | bytes 393224 | tf_op jit(solution)/shard_map/ppermute | solution.py:22
  479.6 7.8 %collective-permute-start.9 = (f32[4,2,1,32,128]{4,3,2,1,0:T(8,128)S(1)}, f32[4,2,1,32,128]{4,3,2,1,0:T(8,128)S(1)}, u32[]{:S(2)}, u32[]{:S(2)}) collective-permute-start(f32[4,2,1,32,128]{4,3,2,1,0:T(8,128)S(1)} %bitcast.76), channel_id=1, source_target_pairs={{0,32},{32,64},{64,96},{1,33},{33,65},{65,97},{2,34},{34,66},{66,9... | collective-permute-start | bytes 393224 | tf_op jit(solution)/shard_map/ppermute | solution.py:20
  481.5 14.5 %copy-start.1 = (f32[4,2,48,32,128]{4,2,3,1,0:T(8,128)S(1)}, f32[4,2,48,32,128]{4,2,3,1,0:T(8,128)}, u32[]{:S(2)}) copy-start(f32[4,2,48,32,128]{4,2,3,1,0:T(8,128)} %copy-done) | copy-start | bytes 18874372
  489.3 13.5 %collective-permute-start.11 = (f32[4,2,50,1,128]{4,2,3,1,0:T(8,128)}, f32[4,2,50,1,128]{4,2,3,1,0:T(8,128)}, u32[]{:S(2)}, u32[]{:S(2)}) collective-permute-start(f32[4,2,50,1,128]{4,2,3,1,0:T(8,128)} %get-tuple-element.17), channel_id=1, source_target_pairs={{0,1},{1,2},{2,3},{4,5},{5,6},{6,7},{8,9},{9,10},{10,11},{12,13},{... | collective-permute-start | bytes 614408 | tf_op jit(solution)/shard_map/ppermute | solution.py:20
  491.2 8.1 %copy-start.4 = (f32[48,32,128]{2,1,0:T(8,128)S(1)}, f32[48,32,128]{2,1,0:T(8,128)}, u32[]{:S(2)}) copy-start(f32[48,32,128]{2,1,0:T(8,128)} %get-tuple-element.35) | copy-start | bytes 2359300
  491.2 11.5 %collective-permute-start.10 = (f32[4,2,50,1,128]{4,2,3,1,0:T(8,128)}, f32[4,2,50,1,128]{4,2,3,1,0:T(8,128)}, u32[]{:S(2)}, u32[]{:S(2)}) collective-permute-start(f32[4,2,50,1,128]{4,2,3,1,0:T(8,128)} %get-tuple-element.16), channel_id=1, source_target_pairs={{1,0},{2,1},{3,2},{5,4},{6,5},{7,6},{9,8},{10,9},{11,10},{13,12},{... | collective-permute-start | bytes 614408 | tf_op jit(solution)/shard_map/ppermute | solution.py:22
Sparse Core Ops, SparseCore 0:
  144.4 51.6 reduce-scatter.3
  226.9 67.7 reduce-scatter.5
  328.2 67.9 reduce-scatter.7
where the time goes:
time: 546 us; the launch traced here: 538 us
  waiting for transfers between devices  212 us (39%)
  blocking collectives  123 us (23%)
  other arithmetic  65.3 us (12%)
  local copies, waits for them, and re-layouts  63.3 us (12%)
  starting transfers between devices  34.3 us (6%)
  matrix products  25.4 us (5%)
  between operations  15 us (3%)
    reduce_scatter x2, waiting for transfers between devices, plane_sine(): lax.psum_scatter(row_blocks, ('slab', 'pois'), scatter_dimension=0, tiled...  134 us
    psum x1, blocking collectives, body(): total = lax.psum(jnp.sum(density_part), ('slab', 'orb', 'pois'))  61.9 us
    all_gather x1, blocking collectives, body(): section = lax.all_gather(field_part, 'orb', axis=2, tiled=True)  61.2 us
    reduce_scatter x1, waiting for transfers between devices, body(): lax.psum_scatter(jnp.einsum('cz,xyz->cxy', sines, density_part, precision...  51.7 us
    sub x2, other arithmetic, taylor_step(): center + time_step * rotated - 0.5 * time_step * time_step * image_two  34.1 us
    ppermute x6, starting transfers between devices, extended(): lax.ppermute(head, axis, [((i + 1) % count, i) for i in range(ends)])  18 us
    ppermute x6, waiting for transfers between devices, extended(): lax.ppermute(tail, axis, [(i, (i + 1) % count) for i in range(ends)])  17.1 us
    ppermute x6, starting transfers between devices, extended(): lax.ppermute(tail, axis, [(i, (i + 1) % count) for i in range(ends)])  16 us
  transfers between devices with their start and end apart: 15, of which 13 were waited for; matrix products, arithmetic and copies ran while one was open for 2% of the time, Pallas kernels for 0%

commit v1 on v0

--- a/solution.py
+++ b/solution.py
@@ -116,7 +116,16 @@
     factor = 32.0 * jnp.pi / ((NX + 1) * (NY + 1) * (NZ + 1))
     scaled = jnp.transpose(spectrum * factor / divisor, (2, 0, 1))
     field_part = plane_sine(scaled)
-    section = lax.all_gather(field_part, "orb", axis=2, tiled=True)
+    list_the_surface = lambda my_data: jnp.concatenate(
+        lax.all_to_all(
+            jnp.stack(lax.axis_size("orb") * [my_data]),
+            axis_name="orb",
+            split_axis=0,
+            concat_axis=0,
+        ),
+        2,
+    )
+    section = list_the_surface(field_part)
     sines = sine_table(full_z, jnp.int32(0), section.shape[2], full_z)
     hartree_full = jnp.einsum("zc,xyc->xyz", sines, section, precision=highest)
     pot_middle = ext_pot + 0.5 * (hartree_old + hartree_full)

time: 546 us -> 510 us (0.934)
  blocking collectives: 123 us -> 76.9 us
  local copies, waits for them, and re-layouts: 63.3 us -> 75.6 us
    all_gather x1 -> x0, blocking collectives: 61.2 us -> none  [body(): section = lax.all_gather(field_part, 'orb', axis=2, tiled=True)]
    all_to_all x0 -> x1, blocking collectives: none -> 14.9 us  [body(): lax.all_to_all(jnp.stack(lax.axis_size('orb') * [my_data]), axis_name='or...]
    unnamed x18 -> x29, local copies, waits for them, and re-layouts: 9.56 us -> 19.3 us
  transfers between devices with their start and end apart: 15 -> 15, of which waited for: 13 -> 12; matrix products, arithmetic and copies ran while one was open for 2% -> 2% of each run, Pallas kernels for 0% -> 0%
where the time goes in v1:
time: 510 us; the launch traced here: 500 us
  waiting for transfers between devices  211 us (41%)
  blocking collectives  76.9 us (15%)
  local copies, waits for them, and re-layouts  75.6 us (15%)
  other arithmetic  66.7 us (13%)
  starting transfers between devices  32 us (6%)
  matrix products  23.2 us (5%)
  between operations  15 us (3%)
    reduce_scatter x2, waiting for transfers between devices, plane_sine(): lax.psum_scatter(row_blocks, ('slab', 'pois'), scatter_dimension=0, tiled...  134 us
    psum x1, blocking collectives, body(): total = lax.psum(jnp.sum(density_part), ('slab', 'orb', 'pois'))  62 us
    reduce_scatter x1, waiting for transfers between devices, body(): lax.psum_scatter(jnp.einsum('cz,xyz->cxy', sines, density_part, precision...  52 us
    sub x2, other arithmetic, taylor_step(): center + time_step * rotated - 0.5 * time_step * time_step * image_two  32.9 us
    unnamed x29, local copies, waits for them, and re-layouts  19.3 us
    ppermute x6, starting transfers between devices, extended(): lax.ppermute(tail, axis, [(i, (i + 1) % count) for i in range(ends)])  17.7 us
    ppermute x6, waiting for transfers between devices, extended(): lax.ppermute(tail, axis, [(i, (i + 1) % count) for i in range(ends)])  17 us
    all_to_all x1, blocking collectives, body(): lax.all_to_all(jnp.stack(lax.axis_size('orb') * [my_data]), axis_name='or...  14.9 us
  transfers between devices with their start and end apart: 15, of which 12 were waited for; matrix products, arithmetic and copies ran while one was open for 2% of the time, Pallas kernels for 0%

profile of v1, /device:TPU:52, one launch (start us, length us, event | category | flops | bytes accessed | tf_op | source)
XLA Modules:
  0.0 500.2 jit_solution(3905920621618041682)
XLA Ops:
  7.2 3.3 fusion.118
  15.4 5.3 %collective-permute-done.1 = bf16[4,2,1,32,128]{4,2,3,1,0:T(2,128)(2,1)S(1)} collective-permute-done((bf16[4,2,1,32,128]{4,2,3,1,0:T(2,128)(2,1)S(1)}, bf16[4,2,1,32,128]{4,2,3,1,0:T(2,128)(2,1)S(1)}, u32[]{:S(2)}, u32[]{:S(2)}) %collective-permute-start.1) | collective-permute-done | bytes 65568 | tf_op jit(solution)/shard_map/ppermute | solution.py:20
  20.7 3.8 collective-permute-start.3
  27.6 3.7 collective-permute-done.2
  31.3 10.8 %multiply_subtract_fusion.1 = (f32[4,2,48,32,128]{4,2,3,1,0:T(8,128)S(1)}, f32[4,2,48,32,128]{4,2,3,1,0:T(8,128)}) fusion(f32[48,32,128]{2,0,1:T(8,128)S(1)} %add_add_fusion.1, bf16[4,2,48,32,128]{4,3,2,1,0:T(8,128)(2,1)S(1)} %copy-done.2, f32[4,2,48,32,128]{4,2,3,1,0:T(8,128)S(1)} %get-tuple-element.33, ...), kind=kLoop, calls=%fused_computation.48 | loop fusion | flops 51904512 | bytes 26288128 | tf_op jit(solution)/shard_map/sub | solution.py:53
  46.7 5.3 %collective-permute-done.5 = f32[4,2,1,32,128]{4,3,2,1,0:T(8,128)S(1)} collective-permute-done((f32[4,2,1,32,128]{4,3,2,1,0:T(8,128)S(1)}, f32[4,2,1,32,128]{4,3,2,1,0:T(8,128)S(1)}, u32[]{:S(2)}, u32[]{:S(2)}) %collective-permute-start.5) | collective-permute-done | bytes 131104 | tf_op jit(solution)/shard_map/ppermute | solution.py:20
  52.1 3.5 collective-permute-start.7
  60.0 3.5 collective-permute-done.6
  63.5 9.9 %fusion.8 = f32[4,2,48,32,128]{4,2,3,1,0:T(8,128)S(1)} fusion(f32[4,2,48,32,128]{4,2,3,1,0:T(8,128)S(1)} %get-tuple-element.14, f32[4,2,50,1,128]{4,2,3,1,0:T(8,128)S(1)} %collective-permute-done.7, f32[4,2,1,32,128]{4,2,3,1,0:T(1,128)S(1)} %bitcast.83, f32[4,2,1,32,128]{4,2,3,1,0:T(1,128)S(1)} %bitcast.85, ...), kind=kLoop, calls=%fused_computation.14 | loop fusion | flops 34603008 | bytes 23478272 | tf_op jit(solution)/shard_map/sub | solution.py:87
  75.6 62.0 %psum.7 = f32[]{:T(128)} all-reduce(f32[]{:T(128)} %get-tuple-element.12), channel_id=1, replica_groups=mesh['slab'=4,'orb'=8,'pois'=4] {'slab','orb','pois'}, use_global_device_ids=true, to_apply=%region_2.3 | all-reduce | flops 1 | bytes 8 | tf_op jit(solution)/shard_map/psum | solution.py:96
  139.7 4.7 fusion.26
  144.4 52.0 %reduce-scatter.4.cloned.1.call-done = f32[16,48,32]{1,0,2:T(8,128)} async-done(((f32[128,48,32]{1,0,2:T(8,128)}), f32[16,48,32]{1,0,2:T(8,128)}) %reduce-scatter.4.cloned.1.call-update) | async-done | bytes 98320 | tf_op jit(solution)/shard_map/reduce_scatter | solution.py:101
  202.0 4.1 convolution_bitcast_fusion.1
  209.1 5.4 %reshape.117 = f32[4,48,4,32,16]{1,0,4,3,2:T(4,128)} reshape(f32[192,128,16]{0,2,1:T(8,128)} %copy.74) | data formatting | bytes 3145728 | tf_op jit(solution)/shard_map/reshape | solution.py:65
  214.5 7.1 %copy.75 = f32[4,4,48,32,16]{3,2,1,0,4:T(8,128)} copy(f32[4,4,48,32,16]{2,0,4,3,1:T(4,128)} %bitcast.75) | data formatting | bytes 3145728 | tf_op jit(solution)/shard_map/transpose | solution.py:66
  221.6 5.6 %reshape.118 = f32[24576,16]{0,1:T(8,128)} reshape(f32[4,4,48,32,16]{3,2,1,0,4:T(8,128)} %copy.75) | data formatting | bytes 3145728 | tf_op jit(solution)/shard_map/reshape | solution.py:66
  228.8 65.8 %reduce-scatter.6.cloned.1.call-done = f32[1536,16]{0,1:T(8,128)} async-done(((f32[24576,16]{0,1:T(8,128)}), f32[1536,16]{0,1:T(8,128)}) %reduce-scatter.6.cloned.1.call-update) | async-done | bytes 98320 | tf_op jit(solution)/shard_map/reduce_scatter | solution.py:67
  302.8 4.1 convolution_bitcast_fusion
  309.9 5.4 %reshape.119 = f32[4,48,4,32,16]{1,0,4,3,2:T(4,128)} reshape(f32[192,128,16]{0,2,1:T(8,128)} %copy.78) | data formatting | bytes 3145728 | tf_op jit(solution)/shard_map/reshape | solution.py:65
  315.3 7.1 %copy.79 = f32[4,4,48,32,16]{3,2,1,0,4:T(8,128)} copy(f32[4,4,48,32,16]{2,0,4,3,1:T(4,128)} %bitcast.76) | data formatting | bytes 3145728 | tf_op jit(solution)/shard_map/transpose | solution.py:66
  322.3 5.6 %reshape.120 = f32[24576,16]{0,1:T(8,128)} reshape(f32[4,4,48,32,16]{3,2,1,0,4:T(8,128)} %copy.79) | data formatting | bytes 3145728 | tf_op jit(solution)/shard_map/reshape | solution.py:66
  328.0 68.1 %reduce-scatter.8.cloned.1.call-done = f32[1536,16]{0,1:T(8,128)} async-done(((f32[24576,16]{0,1:T(8,128)}), f32[1536,16]{0,1:T(8,128)}) %reduce-scatter.8.cloned.1.call-update) | async-done | bytes 98320 | tf_op jit(solution)/shard_map/reduce_scatter | solution.py:67
  400.5 4.0 reshape.126
  404.6 14.9 %all_to_all.5 = f32[8,1,24576]{2,1,0:T(1,128)} all-to-all(f32[8,1,24576]{2,1,0:T(1,128)} %reshape.126), channel_id=1, replica_groups=mesh['slab'=4,'orb'=8,'pois'=4] {'orb'}, dimensions={0} | all-to-all | bytes 1572864 | tf_op jit(solution)/shard_map/all_to_all | solution.py:120
  420.0 4.5 reduce.1
  424.5 3.4 reshape.127
  430.1 5.2 %add_add_fusion = (f32[48,32,128]{2,0,1:T(8,128)S(1)}, f32[48,32,128]{2,0,1:T(8,128)}) fusion(f32[48,32,128]{2,1,0:T(8,128)S(1)} %copy-done.6, f32[48,32,128]{2,1,0:T(8,128)S(1)} %copy-done.8, f32[48,32,128]{0,2,1:T(8,128)S(1)} %bitcast.77, s32[128]{0:T(128)S(1)} %iota_add_fusion.1), kind=kOutput, calls=%fused_computation.71 | convolution fusion | flops 302923776 | bytes 3932672 | tf_op jit(solution)/shard_map/zc,xyc->xyz/dot_general | solution.py:130
  445.5 5.0 collective-permute-done.9
  455.5 3.8 collective-permute-start.10
  459.3 3.3 fusion.113
  465.9 22.9 %fusion.14 = f32[4,2,48,32,128]{4,2,3,1,0:T(8,128)S(1)} fusion(f32[4,2,48,32,128]{4,2,3,1,0:T(8,128)} %copy-done, f32[4,2,50,1,128]{4,2,3,1,0:T(8,128)} %collective-permute-done.11, f32[4,2,1,32,128]{4,2,3,1,0:T(1,128)S(1)} %bitcast.79, f32[4,2,1,32,128]{4,2,3,1,0:T(1,128)S(1)} %bitcast.81, f32[4,2,50,1,128]{4,2,3,1,0:T(8,128)} %collective-permute-done.10, ...), kind=kLoop, calls=%fused_computation.20 | loop fusion | flops 34603008 | bytes 23478272 | tf_op jit(solution)/shard_map/sub | solution.py:87
  488.9 4.6 copy.91
  (82 shorter events, 67.3 us)
Async XLA Ops:
  7.2 189.3 %reduce-scatter.4.cloned.1.call-start = ((), (), s32[]{:S(2)}) async-start(), calls=%async_computation.4 | async-start | bytes 2359296 | tf_op jit(solution)/shard_map/reduce_scatter | solution.py:101
  7.2 19.4 %copy-start.5 = (f32[48,32,128]{2,1,0:T(8,128)S(1)}, f32[48,32,128]{2,1,0:T(8,128)}, u32[]{:S(2)}) copy-start(f32[48,32,128]{2,1,0:T(8,128)} %param.6) | copy-start | bytes 2359300
  7.2 19.4 %copy-start.7 = (f32[48,32,128]{2,1,0:T(8,128)S(1)}, f32[48,32,128]{2,1,0:T(8,128)}, u32[]{:S(2)}) copy-start(f32[48,32,128]{2,1,0:T(8,128)} %param.7) | copy-start | bytes 2359300
  10.5 20.7 %copy-start.2 = (bf16[4,2,48,32,128]{4,3,2,1,0:T(8,128)(2,1)S(1)}, bf16[4,2,48,32,128]{4,3,2,1,0:T(8,128)(2,1)}, u32[]{:S(2)}) copy-start(bf16[4,2,48,32,128]{4,3,2,1,0:T(8,128)(2,1)} %param.4) | copy-start | bytes 9437188
  10.8 4.6 collective-permute-start
  12.9 7.8 %collective-permute-start.1 = (bf16[4,2,1,32,128]{4,2,3,1,0:T(2,128)(2,1)S(1)}, bf16[4,2,1,32,128]{4,2,3,1,0:T(2,128)(2,1)S(1)}, u32[]{:S(2)}, u32[]{:S(2)}) collective-permute-start(bf16[4,2,1,32,128]{4,2,3,1,0:T(2,128)(2,1)S(1)} %get-tuple-element.30), channel_id=1, source_target_pairs={{0,32},{32,64},{64,96},{1,33},{33,65},{65,97},{2,34},{34,66},{66,9... | collective-permute-start | bytes 196616 | tf_op jit(solution)/shard_map/ppermute | solution.py:20
  20.7 6.8 %collective-permute-start.3 = (bf16[4,2,50,1,128]{4,2,3,1,0:T(8,128)(2,1)S(1)}, bf16[4,2,50,1,128]{4,2,3,1,0:T(8,128)(2,1)S(1)}, u32[]{:S(2)}, u32[]{:S(2)}) collective-permute-start(bf16[4,2,50,1,128]{4,2,3,1,0:T(8,128)(2,1)S(1)} %get-tuple-element.29), channel_id=1, source_target_pairs={{0,1},{1,2},{2,3},{4,5},{5,6},{6,7},{8,9},{9,10},{10,11},{12,13},{... | collective-permute-start | bytes 307208 | tf_op jit(solution)/shard_map/ppermute | solution.py:20
  24.6 6.7 %collective-permute-start.2 = (bf16[4,2,50,1,128]{4,2,3,1,0:T(8,128)(2,1)S(1)}, bf16[4,2,50,1,128]{4,2,3,1,0:T(8,128)(2,1)S(1)}, u32[]{:S(2)}, u32[]{:S(2)}) collective-permute-start(bf16[4,2,50,1,128]{4,2,3,1,0:T(8,128)(2,1)S(1)} %get-tuple-element.28), channel_id=1, source_target_pairs={{1,0},{2,1},{3,2},{5,4},{6,5},{7,6},{9,8},{10,9},{11,10},{13,12},{... | collective-permute-start | bytes 307208 | tf_op jit(solution)/shard_map/ppermute | solution.py:22
  42.3 4.4 collective-permute-start.4
  44.2 7.8 %collective-permute-start.5 = (f32[4,2,1,32,128]{4,3,2,1,0:T(8,128)S(1)}, f32[4,2,1,32,128]{4,3,2,1,0:T(8,128)S(1)}, u32[]{:S(2)}, u32[]{:S(2)}) collective-permute-start(f32[4,2,1,32,128]{4,3,2,1,0:T(8,128)S(1)} %bitcast.87), channel_id=1, source_target_pairs={{0,32},{32,64},{64,96},{1,33},{33,65},{65,97},{2,34},{34,66},{66,9... | collective-permute-start | bytes 393224 | tf_op jit(solution)/shard_map/ppermute | solution.py:20
  52.1 7.9 %collective-permute-start.7 = (f32[4,2,50,1,128]{4,2,3,1,0:T(8,128)S(1)}, f32[4,2,50,1,128]{4,2,3,1,0:T(8,128)S(1)}, u32[]{:S(2)}, u32[]{:S(2)}) collective-permute-start(f32[4,2,50,1,128]{4,2,3,1,0:T(8,128)S(1)} %get-tuple-element.19), channel_id=1, source_target_pairs={{0,1},{1,2},{2,3},{4,5},{5,6},{6,7},{8,9},{9,10},{10,11},{12,13},{... | collective-permute-start | bytes 614408 | tf_op jit(solution)/shard_map/ppermute | solution.py:20
  55.6 7.9 %collective-permute-start.6 = (f32[4,2,50,1,128]{4,2,3,1,0:T(8,128)S(1)}, f32[4,2,50,1,128]{4,2,3,1,0:T(8,128)S(1)}, u32[]{:S(2)}, u32[]{:S(2)}) collective-permute-start(f32[4,2,50,1,128]{4,2,3,1,0:T(8,128)S(1)} %get-tuple-element.18), channel_id=1, source_target_pairs={{1,0},{2,1},{3,2},{5,4},{6,5},{7,6},{9,8},{10,9},{11,10},{13,12},{... | collective-permute-start | bytes 614408 | tf_op jit(solution)/shard_map/ppermute | solution.py:22
  63.5 10.0 %copy-start.9 = (f32[4]{0:T(128)S(1)}, f32[4]{0:T(128)}, u32[]{:S(2)}) copy-start(f32[4]{0:T(128)} %param.5) | copy-start | bytes 52
  144.4 150.3 %reduce-scatter.6.cloned.1.call-start = ((), (), s32[]{:S(2)}) async-start(), calls=%async_computation.5 | async-start | bytes 1671168 | tf_op jit(solution)/shard_map/reduce_scatter | solution.py:67
  227.2 168.9 %reduce-scatter.8.cloned.1.call-start = ((), (), s32[]{:S(2)}) async-start(), calls=%async_computation.6 | async-start | bytes 1671168 | tf_op jit(solution)/shard_map/reduce_scatter | solution.py:67
  427.9 2.2 copy-start.6
  427.9 2.2 copy-start.8
  427.9 7.4 %slice-start = ((s8[6291456]{0:T(1024)(128)(4,1)}), s8[4194304]{0:T(1024)(128)(4,1)S(1)}, s32[]{:S(2)}) async-start(s8[6291456]{0:T(1024)(128)(4,1)} %bitcast.73), calls=%async_computation.7 | async-start | bytes 8388608
  429.8 5.5 %slice-start.1 = ((s8[6291456]{0:T(1024)(128)(4,1)}), s8[2097152]{0:T(1024)(128)(4,1)S(1)}, s32[]{:S(2)}) async-start(s8[6291456]{0:T(1024)(128)(4,1)} %bitcast.73), calls=%async_computation.8 | async-start | bytes 4194304
  435.3 1.8 copy-start.3
  437.2 2.7 copy-start
  440.8 4.7 collective-permute-start.8
  442.7 7.8 %collective-permute-start.9 = (f32[4,2,1,32,128]{4,3,2,1,0:T(8,128)S(1)}, f32[4,2,1,32,128]{4,3,2,1,0:T(8,128)S(1)}, u32[]{:S(2)}, u32[]{:S(2)}) collective-permute-start(f32[4,2,1,32,128]{4,3,2,1,0:T(8,128)S(1)} %bitcast.86), channel_id=1, source_target_pairs={{0,32},{32,64},{64,96},{1,33},{33,65},{65,97},{2,34},{34,66},{66,9... | collective-permute-start | bytes 393224 | tf_op jit(solution)/shard_map/ppermute | solution.py:20
  445.1 14.2 %copy-start.1 = (f32[4,2,48,32,128]{4,2,3,1,0:T(8,128)S(1)}, f32[4,2,48,32,128]{4,2,3,1,0:T(8,128)}, u32[]{:S(2)}) copy-start(f32[4,2,48,32,128]{4,2,3,1,0:T(8,128)} %copy-done) | copy-start | bytes 18874372
  452.4 13.6 %collective-permute-start.11 = (f32[4,2,50,1,128]{4,2,3,1,0:T(8,128)}, f32[4,2,50,1,128]{4,2,3,1,0:T(8,128)}, u32[]{:S(2)}, u32[]{:S(2)}) collective-permute-start(f32[4,2,50,1,128]{4,2,3,1,0:T(8,128)} %get-tuple-element.17), channel_id=1, source_target_pairs={{0,1},{1,2},{2,3},{4,5},{5,6},{6,7},{8,9},{9,10},{10,11},{12,13},{... | collective-permute-start | bytes 614408 | tf_op jit(solution)/shard_map/ppermute | solution.py:20
  455.5 7.1 %copy-start.4 = (f32[48,32,128]{2,0,1:T(8,128)S(1)}, f32[48,32,128]{2,0,1:T(8,128)}, u32[]{:S(2)}) copy-start(f32[48,32,128]{2,0,1:T(8,128)} %get-tuple-element.35) | copy-start | bytes 2359300
  455.5 10.4 %collective-permute-start.10 = (f32[4,2,50,1,128]{4,2,3,1,0:T(8,128)}, f32[4,2,50,1,128]{4,2,3,1,0:T(8,128)}, u32[]{:S(2)}, u32[]{:S(2)}) collective-permute-start(f32[4,2,50,1,128]{4,2,3,1,0:T(8,128)} %get-tuple-element.16), channel_id=1, source_target_pairs={{1,0},{2,1},{3,2},{5,4},{6,5},{7,6},{9,8},{10,9},{11,10},{13,12},{... | collective-permute-start | bytes 614408 | tf_op jit(solution)/shard_map/ppermute | solution.py:22
Sparse Core Ops, SparseCore 0:
  144.5 51.9 reduce-scatter.3
  227.3 67.2 reduce-scatter.5
  328.1 67.9 reduce-scatter.7
